TPU v7x, 256 devices: a whole 4x4x8 slice. The times are simulated.
256 devices in a mesh: lat: 8 (over z), lon: 32 (over x, y, core).
Axes of the slice: x: 4, y: 4, z: 8, core: 2. Of those that a mesh axis runs over, the one named last changes fastest.
Arguments:
- inputs: bfloat16 [4, 128, 256, 1024], P(None, 'lat', 'lon'), may hold values from -6 to 6
- w_reduce: bfloat16 [1024, 256], replicated, may hold values from -0.1875 to 0.1875
- gain_reduce: float32 [256], replicated, may hold values from 0.1 to 1.9
- bias_reduce: float32 [256], replicated, may hold values from -3 to 3
- w_dilated: bfloat16 [3, 3, 256, 256], replicated, may hold values from -0.125 to 0.125
- gain_dilated: float32 [256], replicated, may hold values from 0.1 to 1.9
- bias_dilated: float32 [256], replicated, may hold values from -3 to 3
- w_expand: bfloat16 [256, 1024], replicated, may hold values from -0.375 to 0.375
- gain_expand: float32 [1024], replicated, may hold values from 0.1 to 1.9
- bias_expand: float32 [1024], replicated, may hold values from -3 to 3
- grad_out: bfloat16 [4, 128, 256, 1024], P(None, 'lat', 'lon'), may hold values from -6 to 6
- labels: int32 [4, 128, 256], P(None, 'lat', 'lon'), may hold values from 0 to 2
- class_weight: float32 [3], replicated, may hold values from 0.5 to 8
Outputs:
- grad_inputs: bfloat16 [4, 128, 256, 1024], P(None, 'lat', 'lon')
- grad_reduce: bfloat16 [1024, 256], replicated
- grad_dilated: bfloat16 [3, 3, 256, 256], replicated
- grad_expand: bfloat16 [256, 1024], replicated
All inputs are finite; a program needn't handle non-finite values.
Results may differ from a plain program's by a relative error of at most 0.0079.
Values may be sent and summed in bfloat16 or wider, within the bound.
A program may use at most 64 MiB of HBM per device.

v0:
```python
import jax
import jax.numpy as jnp
from jax import lax
from jax.sharding import PartitionSpec as P


def with_halo(cells, sides, width, closed):
    for axis, dim in sides:
        count = lax.axis_size(axis)
        ends = count if closed else count - 1
        head = lax.slice_in_dim(cells, 0, width, axis=dim)
        tail = lax.slice_in_dim(cells, cells.shape[dim] - width, cells.shape[dim], axis=dim)
        cells = jnp.concatenate(
            [
                lax.ppermute(tail, axis, [(i, (i + 1) % count) for i in range(ends)]),
                cells,
                lax.ppermute(head, axis, [((i + 1) % count, i) for i in range(ends)]),
            ],
            axis=dim,
        )
    return cells


def smooth(pre):
    return pre * jax.nn.sigmoid(pre)


def slope(pre):
    sig = jax.nn.sigmoid(pre)
    return sig * (1.0 + pre * (1.0 - sig))


def gather_taps(padded, height, width, flipped):
    pieces = []
    for row_tap in range(3):
        for col_tap in range(3):
            off_row = 4 - 2 * row_tap if flipped else 2 * row_tap
            off_col = 4 - 2 * col_tap if flipped else 2 * col_tap
            pieces.append(padded[:, off_row : off_row + height, off_col : off_col + width, :])
    stacked = jnp.concatenate(pieces, axis=-1)
    return stacked.reshape(-1, stacked.shape[-1])


def pixel_sum(left, right):
    return lax.dot_general(
        left, right, (((0,), (0,)), ((), ())), preferred_element_type=jnp.float32
    )


def per_device(
    inputs,
    w_reduce,
    gain_reduce,
    bias_reduce,
    w_dilated,
    gain_dilated,
    bias_dilated,
    w_expand,
    gain_expand,
    bias_expand,
    grad_out,
    labels,
    class_weight,
):
    batch, height, width, chan_in = inputs.shape
    chan_mid = w_reduce.shape[1]
    pixels = batch * height * width
    kernel = w_dilated.reshape(9 * chan_mid, chan_mid)
    kernel_back = jnp.transpose(w_dilated, (0, 1, 3, 2)).reshape(9 * chan_mid, chan_mid)
    classes = jnp.arange(class_weight.shape[0], dtype=jnp.int32)
    flat_in = inputs.reshape(pixels, chan_in)
    pre_one = (
        jnp.dot(flat_in, w_reduce, preferred_element_type=jnp.float32) * gain_reduce + bias_reduce
    )
    mid_one = smooth(pre_one).astype(jnp.bfloat16).reshape(batch, height, width, chan_mid)
    rows_one = with_halo(mid_one, (("lat", 1),), 2, False)
    padded_one = with_halo(rows_one, (("lon", 2),), 2, True)
    taps_one = gather_taps(padded_one, height, width, False)
    pre_two = (
        jnp.dot(taps_one, kernel, preferred_element_type=jnp.float32) * gain_dilated + bias_dilated
    )
    mid_two = smooth(pre_two).astype(jnp.bfloat16)
    pre_three = (
        jnp.dot(mid_two, w_expand, preferred_element_type=jnp.float32) * gain_expand
        + bias_expand
        + flat_in.astype(jnp.float32)
    )
    pixel_weight = jnp.sum(
        jnp.where(labels.reshape(pixels, 1) == classes, class_weight, 0.0), axis=-1
    )
    grad_full = (
        grad_out.reshape(pixels, chan_in).astype(jnp.float32)
        * pixel_weight[:, None]
        * slope(pre_three)
    )
    grad_three = (grad_full * gain_expand).astype(jnp.bfloat16)
    term_expand = pixel_sum(mid_two, grad_three)
    grad_two = (
        jnp.dot(grad_three, w_expand.T, preferred_element_type=jnp.float32)
        * slope(pre_two)
        * gain_dilated
    ).astype(jnp.bfloat16)
    term_dilated = pixel_sum(taps_one, grad_two)
    rows_two = with_halo(grad_two.reshape(batch, height, width, chan_mid), (("lat", 1),), 2, False)
    padded_two = with_halo(rows_two, (("lon", 2),), 2, True)
    taps_two = gather_taps(padded_two, height, width, True)
    grad_one = (
        jnp.dot(taps_two, kernel_back, preferred_element_type=jnp.float32)
        * slope(pre_one)
        * gain_reduce
    ).astype(jnp.bfloat16)
    term_reduce = pixel_sum(flat_in, grad_one)
    grad_inputs = (
        jnp.dot(grad_one, w_reduce.T, preferred_element_type=jnp.float32) + grad_full
    ).astype(jnp.bfloat16)
    total_reduce, total_dilated, total_expand = lax.psum(
        (term_reduce, term_dilated, term_expand), ("lat", "lon")
    )
    grad_reduce = total_reduce.astype(jnp.bfloat16)
    grad_dilated = total_dilated.astype(jnp.bfloat16)
    grad_expand = total_expand.astype(jnp.bfloat16)
    grad_dilated = grad_dilated.reshape(3, 3, chan_mid, chan_mid)
    return (
        grad_inputs.reshape(batch, height, width, chan_in),
        grad_reduce,
        grad_dilated,
        grad_expand,
    )


def solution(mesh):
    return jax.shard_map(
        per_device,
        mesh=mesh,
        in_specs=(
            P(None, "lat", "lon", None),
            P(),
            P(),
            P(),
            P(),
            P(),
            P(),
            P(),
            P(),
            P(),
            P(None, "lat", "lon", None),
            P(None, "lat", "lon"),
            P(),
        ),
        out_specs=(P(None, "lat", "lon", None), P(), P(), P()),
        check_vma=False,
    )
```

profile of v0, /device:TPU:64, one launch (start us, length us, event | category | flops | bytes accessed | tf_op | source)
XLA Modules:
  0.0 187.6 jit_solution(14700682848667514248)
XLA Ops:
  0.6 0.0 copy-start
  0.6 1.0 copy-done
  1.7 1.8 multiply_convert_fusion.2
  3.5 3.8 %collective-permute-start = (bf16[4,2,8,256]{3,2,1,0:T(8,128)(2,1)S(1)}, bf16[4,2,8,256]{3,2,1,0:T(8,128)(2,1)S(1)}, u32[]{:S(2)}, u32[]{:S(2)}) collective-permute-start(bf16[4,2,8,256]{3,2,1,0:T(8,128)(2,1)S(1)} %get-tuple-element.45), channel_id=1, source_target_pairs={{0,32},{32,64},{64,96},{96,128},{128,160},{160,192},{192,224},{1,3... | collective-permute-start | bytes 98312 | tf_op jit(solution)/shard_map/ppermute | solution.py:15
  7.3 2.0 %collective-permute-start.1 = (bf16[4,2,8,256]{3,2,1,0:T(8,128)(2,1)S(1)}, bf16[4,2,8,256]{3,2,1,0:T(8,128)(2,1)S(1)}, u32[]{:S(2)}, u32[]{:S(2)}) collective-permute-start(bf16[4,2,8,256]{3,2,1,0:T(8,128)(2,1)S(1)} %get-tuple-element.46), channel_id=1, source_target_pairs={{32,0},{64,32},{96,64},{128,96},{160,128},{192,160},{224,192},{33,... | collective-permute-start | bytes 98312 | tf_op jit(solution)/shard_map/ppermute | solution.py:17
  9.4 0.1 copy.21
  9.5 0.1 eq.15
  9.6 0.1 select_reduce_fusion
  9.6 1.5 copy.22
  11.2 0.0 collective-permute-done
  11.2 3.1 %collective-permute-done.1 = bf16[4,2,8,256]{3,2,1,0:T(8,128)(2,1)S(1)} collective-permute-done((bf16[4,2,8,256]{3,2,1,0:T(8,128)(2,1)S(1)}, bf16[4,2,8,256]{3,2,1,0:T(8,128)(2,1)S(1)}, u32[]{:S(2)}, u32[]{:S(2)}) %collective-permute-start.1) | collective-permute-done | bytes 32800 | tf_op jit(solution)/shard_map/ppermute | solution.py:17
  14.3 0.1 pad_maximum_fusion.9
  14.4 0.1 collective-permute-start.2
  14.5 5.1 %collective-permute-start.3 = (bf16[4,20,2,256]{3,2,1,0:T(2,128)(2,1)S(1)}, bf16[4,20,2,256]{3,2,1,0:T(2,128)(2,1)S(1)}, u32[]{:S(2)}, u32[]{:S(2)}) collective-permute-start(bf16[4,20,2,256]{3,2,1,0:T(2,128)(2,1)S(1)} %get-tuple-element.37), channel_id=1, source_target_pairs={{1,0},{2,1},{3,2},{4,3},{5,4},{6,5},{7,6},{8,7},{9,8},{10,9},{11,1... | collective-permute-start | bytes 245768 | tf_op jit(solution)/shard_map/ppermute | solution.py:17
  19.6 2.1 %collective-permute-done.2 = bf16[4,20,2,256]{3,2,1,0:T(2,128)(2,1)S(1)} collective-permute-done((bf16[4,20,2,256]{3,2,1,0:T(2,128)(2,1)S(1)}, bf16[4,20,2,256]{3,2,1,0:T(2,128)(2,1)S(1)}, u32[]{:S(2)}, u32[]{:S(2)}) %collective-permute-start.2) | collective-permute-done | bytes 81952 | tf_op jit(solution)/shard_map/ppermute | solution.py:15
  21.6 0.4 pad_maximum_fusion
  22.0 0.2 fusion.10
  22.2 0.0 copy-start.10
  22.2 0.0 copy-start.11
  22.5 0.4 copy-done.10
  22.9 0.0 copy-done.11
  22.9 0.0 copy-start.9
  22.9 0.8 fusion.2
  23.7 0.4 copy-done.3
  24.1 0.3 copy-done.7
  24.5 0.1 copy-done.8
  24.6 1.3 fusion
  25.9 0.5 fusion.6
  26.4 0.8 fusion.14
  27.3 5.1 %collective-permute-start.4 = (bf16[4,2,8,256]{3,2,1,0:T(8,128)(2,1)S(1)}, bf16[4,2,8,256]{3,2,1,0:T(8,128)(2,1)S(1)}, u32[]{:S(2)}, u32[]{:S(2)}) collective-permute-start(bf16[4,2,8,256]{3,2,1,0:T(8,128)(2,1)S(1)} %get-tuple-element.41), channel_id=1, source_target_pairs={{0,32},{32,64},{64,96},{96,128},{128,160},{160,192},{192,224},{1,3... | collective-permute-start | bytes 98312 | tf_op jit(solution)/shard_map/ppermute | solution.py:15
  32.4 1.9 %collective-permute-start.5 = (bf16[4,2,8,256]{3,2,1,0:T(8,128)(2,1)S(1)}, bf16[4,2,8,256]{3,2,1,0:T(8,128)(2,1)S(1)}, u32[]{:S(2)}, u32[]{:S(2)}) collective-permute-start(bf16[4,2,8,256]{3,2,1,0:T(8,128)(2,1)S(1)} %get-tuple-element.42), channel_id=1, source_target_pairs={{32,0},{64,32},{96,64},{128,96},{160,128},{192,160},{224,192},{33,... | collective-permute-start | bytes 98312 | tf_op jit(solution)/shard_map/ppermute | solution.py:17
  34.3 1.5 fusion.7
  35.8 2.4 %collective-permute-done.5 = bf16[4,2,8,256]{3,2,1,0:T(8,128)(2,1)S(1)} collective-permute-done((bf16[4,2,8,256]{3,2,1,0:T(8,128)(2,1)S(1)}, bf16[4,2,8,256]{3,2,1,0:T(8,128)(2,1)S(1)}, u32[]{:S(2)}, u32[]{:S(2)}) %collective-permute-start.5) | collective-permute-done | bytes 32800 | tf_op jit(solution)/shard_map/ppermute | solution.py:17
  38.2 0.1 pad_maximum_fusion.6
  38.3 3.7 %collective-permute-start.6 = (bf16[4,20,2,256]{3,2,1,0:T(2,128)(2,1)S(1)}, bf16[4,20,2,256]{3,2,1,0:T(2,128)(2,1)S(1)}, u32[]{:S(2)}, u32[]{:S(2)}) collective-permute-start(bf16[4,20,2,256]{3,2,1,0:T(2,128)(2,1)S(1)} %get-tuple-element.34), channel_id=1, source_target_pairs={{1,0},{2,1},{3,2},{4,3},{5,4},{6,5},{7,6},{8,7},{9,8},{10,9},{11,1... | collective-permute-start | bytes 245768 | tf_op jit(solution)/shard_map/ppermute | solution.py:17
  42.1 2.0 %collective-permute-done.6 = bf16[4,20,2,256]{3,2,1,0:T(2,128)(2,1)S(1)} collective-permute-done((bf16[4,20,2,256]{3,2,1,0:T(2,128)(2,1)S(1)}, bf16[4,20,2,256]{3,2,1,0:T(2,128)(2,1)S(1)}, u32[]{:S(2)}, u32[]{:S(2)}) %collective-permute-start.6) | collective-permute-done | bytes 81952 | tf_op jit(solution)/shard_map/ppermute | solution.py:17
  44.1 5.1 %collective-permute-done.7 = bf16[4,20,2,256]{3,2,1,0:T(2,128)(2,1)S(1)} collective-permute-done((bf16[4,20,2,256]{3,2,1,0:T(2,128)(2,1)S(1)}, bf16[4,20,2,256]{3,2,1,0:T(2,128)(2,1)S(1)}, u32[]{:S(2)}, u32[]{:S(2)}) %collective-permute-start.7) | collective-permute-done | bytes 81952 | tf_op jit(solution)/shard_map/ppermute | solution.py:15
  49.2 0.4 maximum_maximum_fusion.1
  49.6 0.1 fusion.9
  49.8 0.1 fusion.8
  49.8 0.0 copy-start.2
  49.9 0.0 copy-start.12
  50.1 1.0 copy-done.2
  51.1 0.8 fusion.5
  51.9 1.5 convolution_bitcast_fusion
  53.4 1.5 add_convert_fusion
  54.8 131.7 %all-reduce.2 = (bf16[1024,256]{0,1:T(8,128)(2,1)S(1)}, bf16[2304,256]{1,0:T(8,128)(2,1)}, bf16[256,1024]{1,0:T(8,128)(2,1)}) all-reduce(f32[1024,256]{0,1:T(8,128)} %convolution_bitcast_fusion, f32[2304,256]{1,0:T(8,128)S(1)} %fusion.14, f32[256,1024]{1,0:T(8,128)} %fusion.7), channel_id=1, replica_groups=mesh['lat'=8,'lon'=32] {'lat','lon'}, use_global_device_ids=true, to_apply=%region_1.2 | all-reduce | flops 1114112 | bytes 6684672 | tf_op jit(solution)/shard_map/psum | solution.py:116
  186.6 1.0 copy.23
  (38 shorter events, 0.5 us)
Async XLA Ops:
  0.6 1.0 copy-start
  1.7 7.7 %copy-start.4 = (s32[4,16,8]{1,2,0:T(8,128)S(1)}, s32[4,16,8]{1,2,0:T(8,128)}, u32[]{:S(2)}) copy-start(s32[4,16,8]{1,2,0:T(8,128)} %param.24) | copy-start | bytes 6148
  1.7 7.9 %copy-start.6 = (f32[3]{0:T(128)S(1)}, f32[3]{0:T(128)}, u32[]{:S(2)}) copy-start(f32[3]{0:T(128)} %param.25) | copy-start | bytes 40
  1.7 8.0 %copy-start.1 = (bf16[3,3,256,256]{3,2,1,0:T(8,128)(2,1)S(1)}, bf16[3,3,256,256]{3,2,1,0:T(8,128)(2,1)}, u32[]{:S(2)}) copy-start(bf16[3,3,256,256]{3,2,1,0:T(8,128)(2,1)} %param.17) | copy-start | bytes 3538948
  3.5 7.7 %collective-permute-start = (bf16[4,2,8,256]{3,2,1,0:T(8,128)(2,1)S(1)}, bf16[4,2,8,256]{3,2,1,0:T(8,128)(2,1)S(1)}, u32[]{:S(2)}, u32[]{:S(2)}) collective-permute-start(bf16[4,2,8,256]{3,2,1,0:T(8,128)(2,1)S(1)} %get-tuple-element.45), channel_id=1, source_target_pairs={{0,32},{32,64},{64,96},{96,128},{128,160},{160,192},{192,224},{1,3... | collective-permute-start | bytes 98312 | tf_op jit(solution)/shard_map/ppermute | solution.py:15
  7.3 6.9 %collective-permute-start.1 = (bf16[4,2,8,256]{3,2,1,0:T(8,128)(2,1)S(1)}, bf16[4,2,8,256]{3,2,1,0:T(8,128)(2,1)S(1)}, u32[]{:S(2)}, u32[]{:S(2)}) collective-permute-start(bf16[4,2,8,256]{3,2,1,0:T(8,128)(2,1)S(1)} %get-tuple-element.46), channel_id=1, source_target_pairs={{32,0},{64,32},{96,64},{128,96},{160,128},{192,160},{224,192},{33,... | collective-permute-start | bytes 98312 | tf_op jit(solution)/shard_map/ppermute | solution.py:17
  14.4 7.3 %collective-permute-start.2 = (bf16[4,20,2,256]{3,2,1,0:T(2,128)(2,1)S(1)}, bf16[4,20,2,256]{3,2,1,0:T(2,128)(2,1)S(1)}, u32[]{:S(2)}, u32[]{:S(2)}) collective-permute-start(bf16[4,20,2,256]{3,2,1,0:T(2,128)(2,1)S(1)} %get-tuple-element.38), channel_id=1, source_target_pairs={{0,1},{1,2},{2,3},{3,4},{4,5},{5,6},{6,7},{7,8},{8,9},{9,10},{10,1... | collective-permute-start | bytes 245768 | tf_op jit(solution)/shard_map/ppermute | solution.py:15
  14.5 7.2 %collective-permute-start.3 = (bf16[4,20,2,256]{3,2,1,0:T(2,128)(2,1)S(1)}, bf16[4,20,2,256]{3,2,1,0:T(2,128)(2,1)S(1)}, u32[]{:S(2)}, u32[]{:S(2)}) collective-permute-start(bf16[4,20,2,256]{3,2,1,0:T(2,128)(2,1)S(1)} %get-tuple-element.37), channel_id=1, source_target_pairs={{1,0},{2,1},{3,2},{4,3},{5,4},{6,5},{7,6},{8,7},{9,8},{10,9},{11,1... | collective-permute-start | bytes 245768 | tf_op jit(solution)/shard_map/ppermute | solution.py:17
  22.2 0.7 copy-start.10
  22.2 0.7 copy-start.11
  22.9 1.2 copy-start.3
  22.9 1.2 copy-start.5
  22.9 1.6 copy-start.7
  22.9 1.7 copy-start.8
  22.9 1.7 copy-start.9
  27.3 8.6 %collective-permute-start.4 = (bf16[4,2,8,256]{3,2,1,0:T(8,128)(2,1)S(1)}, bf16[4,2,8,256]{3,2,1,0:T(8,128)(2,1)S(1)}, u32[]{:S(2)}, u32[]{:S(2)}) collective-permute-start(bf16[4,2,8,256]{3,2,1,0:T(8,128)(2,1)S(1)} %get-tuple-element.41), channel_id=1, source_target_pairs={{0,32},{32,64},{64,96},{96,128},{128,160},{160,192},{192,224},{1,3... | collective-permute-start | bytes 98312 | tf_op jit(solution)/shard_map/ppermute | solution.py:15
  32.4 5.8 %collective-permute-start.5 = (bf16[4,2,8,256]{3,2,1,0:T(8,128)(2,1)S(1)}, bf16[4,2,8,256]{3,2,1,0:T(8,128)(2,1)S(1)}, u32[]{:S(2)}, u32[]{:S(2)}) collective-permute-start(bf16[4,2,8,256]{3,2,1,0:T(8,128)(2,1)S(1)} %get-tuple-element.42), channel_id=1, source_target_pairs={{32,0},{64,32},{96,64},{128,96},{160,128},{192,160},{224,192},{33,... | collective-permute-start | bytes 98312 | tf_op jit(solution)/shard_map/ppermute | solution.py:17
  38.3 5.8 %collective-permute-start.6 = (bf16[4,20,2,256]{3,2,1,0:T(2,128)(2,1)S(1)}, bf16[4,20,2,256]{3,2,1,0:T(2,128)(2,1)S(1)}, u32[]{:S(2)}, u32[]{:S(2)}) collective-permute-start(bf16[4,20,2,256]{3,2,1,0:T(2,128)(2,1)S(1)} %get-tuple-element.34), channel_id=1, source_target_pairs={{1,0},{2,1},{3,2},{4,3},{5,4},{6,5},{7,6},{8,7},{9,8},{10,9},{11,1... | collective-permute-start | bytes 245768 | tf_op jit(solution)/shard_map/ppermute | solution.py:17
  42.0 7.2 %collective-permute-start.7 = (bf16[4,20,2,256]{3,2,1,0:T(2,128)(2,1)S(1)}, bf16[4,20,2,256]{3,2,1,0:T(2,128)(2,1)S(1)}, u32[]{:S(2)}, u32[]{:S(2)}) collective-permute-start(bf16[4,20,2,256]{3,2,1,0:T(2,128)(2,1)S(1)} %get-tuple-element.33), channel_id=1, source_target_pairs={{0,1},{1,2},{2,3},{3,4},{4,5},{5,6},{6,7},{7,8},{8,9},{9,10},{10,1... | collective-permute-start | bytes 245768 | tf_op jit(solution)/shard_map/ppermute | solution.py:15
  49.8 1.3 copy-start.2
  49.9 1.3 copy-start.12
where the time goes:
time: 188 us
  blocking collectives  132 us (70%)
  starting transfers between devices  21.7 us (12%)
  waiting for transfers between devices  14.7 us (8%)
  matrix products  10.4 us (6%)
  local copies, waits for them, and re-layouts  6.82 us (4%)
    psum x1, blocking collectives, per_device(): lax.psum((term_reduce, term_dilated, term_expand), ('lat', 'lon'))  132 us
    ppermute x4, starting transfers between devices, with_halo(): lax.ppermute(head, axis, [((i + 1) % count, i) for i in range(ends)])  12.7 us
    ppermute x4, starting transfers between devices, with_halo(): lax.ppermute(tail, axis, [(i, (i + 1) % count) for i in range(ends)])  9.04 us
    ppermute x4, waiting for transfers between devices, with_halo(): lax.ppermute(head, axis, [((i + 1) % count, i) for i in range(ends)])  7.49 us
    ppermute x4, waiting for transfers between devices, with_halo(): lax.ppermute(tail, axis, [(i, (i + 1) % count) for i in range(ends)])  7.21 us
    unnamed x45, local copies, waits for them, and re-layouts  6.35 us
    dot_general x3, matrix products, pixel_sum(): lax.dot_general(left, right, (((0,), (0,)), ((), ())), preferred_element_...  3.79 us
  transfers between devices with their start and end apart: 8, of which 5 were waited for; matrix products, arithmetic and copies ran while one was open for 2% of the time, Pallas kernels for 0%

commit v1 on v0

--- a/solution.py
+++ b/solution.py
@@ -2,6 +2,7 @@
 import jax.numpy as jnp
 from jax import lax
 from jax.sharding import PartitionSpec as P
+from jax.lax import psum
 
 
 def with_halo(cells, sides, width, closed):
@@ -113,8 +114,12 @@
     grad_inputs = (
         jnp.dot(grad_one, w_reduce.T, preferred_element_type=jnp.float32) + grad_full
     ).astype(jnp.bfloat16)
-    total_reduce, total_dilated, total_expand = lax.psum(
-        (term_reduce, term_dilated, term_expand), ("lat", "lon")
+
+    def edit_the_stacks_all(own_rows):
+        return psum(psum(own_rows, "lon"), "lat")
+
+    total_reduce, total_dilated, total_expand = edit_the_stacks_all(
+        (term_reduce, term_dilated, term_expand)
     )
     grad_reduce = total_reduce.astype(jnp.bfloat16)
     grad_dilated = total_dilated.astype(jnp.bfloat16)

time: 188 us -> 283 us (1.51)
  waiting for transfers between devices: 14.7 us -> 130 us
  blocking collectives: 132 us -> 94.3 us
  between operations: 1 us -> 14.4 us
    psum x0 -> x1, waiting for transfers between devices: none -> 116 us  [edit_the_stacks_all(): return psum(psum(own_rows, 'lon'), 'lat')]
    psum x1, blocking collectives: 132 us -> 94.3 us  [edit_the_stacks_all(): return psum(psum(own_rows, 'lon'), 'lat')]
  transfers between devices with their start and end apart: 8 -> 9, of which waited for: 5 -> 6; matrix products, arithmetic and copies ran while one was open for 2% -> 2% of each run, Pallas kernels for 0% -> 0%
where the time goes in v1:
time: 283 us; the launch traced here: 280 us
  waiting for transfers between devices  130 us (46%)
  blocking collectives  94.3 us (33%)
  starting transfers between devices  21.8 us (8%)
  between operations  14.4 us (5%)
  matrix products  11.8 us (4%)
  local copies, waits for them, and re-layouts  6.77 us (2%)
    psum x1, waiting for transfers between devices, edit_the_stacks_all(): return psum(psum(own_rows, 'lon'), 'lat')  116 us
    psum x1, blocking collectives, edit_the_stacks_all(): return psum(psum(own_rows, 'lon'), 'lat')  94.3 us
    ppermute x4, starting transfers between devices, with_halo(): lax.ppermute(head, axis, [((i + 1) % count, i) for i in range(ends)])  12.7 us
    ppermute x4, starting transfers between devices, with_halo(): lax.ppermute(tail, axis, [(i, (i + 1) % count) for i in range(ends)])  9.03 us
    ppermute x4, waiting for transfers between devices, with_halo(): lax.ppermute(head, axis, [((i + 1) % count, i) for i in range(ends)])  7.49 us
    ppermute x4, waiting for transfers between devices, with_halo(): lax.ppermute(tail, axis, [(i, (i + 1) % count) for i in range(ends)])  7.21 us
    unnamed x45, local copies, waits for them, and re-layouts  6.31 us
  transfers between devices with their start and end apart: 9, of which 6 were waited for; matrix products, arithmetic and copies ran while one was open for 2% of the time, Pallas kernels for 0%

profile of v1, /device:TPU:64, one launch (start us, length us, event | category | flops | bytes accessed | tf_op | source)
XLA Modules:
  0.0 280.4 jit_solution(12945968359879216007)
XLA Ops:
  7.2 0.0 copy-start
  7.2 0.0 all-reduce.5.cloned.1.call-start
  7.2 1.0 copy-done
  8.2 1.8 multiply_convert_fusion.2
  10.0 3.8 %collective-permute-start = (bf16[4,2,8,256]{3,2,1,0:T(8,128)(2,1)S(1)}, bf16[4,2,8,256]{3,2,1,0:T(8,128)(2,1)S(1)}, u32[]{:S(2)}, u32[]{:S(2)}) collective-permute-start(bf16[4,2,8,256]{3,2,1,0:T(8,128)(2,1)S(1)} %get-tuple-element.48), channel_id=1, source_target_pairs={{0,32},{32,64},{64,96},{96,128},{128,160},{160,192},{192,224},{1,3... | collective-permute-start | bytes 98312 | tf_op jit(solution)/shard_map/ppermute | solution.py:16
  13.9 2.0 collective-permute-start.1
  15.9 0.1 copy.21
  16.0 0.1 eq.15
  16.1 0.1 select_reduce_fusion
  16.2 1.5 copy.22
  17.7 3.1 %collective-permute-done.1 = bf16[4,2,8,256]{3,2,1,0:T(8,128)(2,1)S(1)} collective-permute-done((bf16[4,2,8,256]{3,2,1,0:T(8,128)(2,1)S(1)}, bf16[4,2,8,256]{3,2,1,0:T(8,128)(2,1)S(1)}, u32[]{:S(2)}, u32[]{:S(2)}) %collective-permute-start.1) | collective-permute-done | bytes 32800 | tf_op jit(solution)/shard_map/ppermute | solution.py:18
  20.8 0.1 pad_maximum_fusion.9
  20.9 0.1 collective-permute-start.2
  21.0 5.1 %collective-permute-start.3 = (bf16[4,20,2,256]{3,2,1,0:T(2,128)(2,1)S(1)}, bf16[4,20,2,256]{3,2,1,0:T(2,128)(2,1)S(1)}, u32[]{:S(2)}, u32[]{:S(2)}) collective-permute-start(bf16[4,20,2,256]{3,2,1,0:T(2,128)(2,1)S(1)} %get-tuple-element.40), channel_id=1, source_target_pairs={{1,0},{2,1},{3,2},{4,3},{5,4},{6,5},{7,6},{8,7},{9,8},{10,9},{11,1... | collective-permute-start | bytes 245768 | tf_op jit(solution)/shard_map/ppermute | solution.py:18
  26.1 2.1 collective-permute-done.2
  28.2 0.4 pad_maximum_fusion
  28.5 0.2 fusion.10
  28.7 0.0 copy-start.10
  29.0 0.4 copy-done.10
  29.4 0.0 copy-done.11
  29.5 0.0 copy-start.9
  29.5 0.8 fusion.2
  30.3 0.4 copy-done.3
  30.7 0.3 copy-done.7
  31.0 0.1 copy-done.8
  31.1 1.3 fusion
  32.4 0.5 fusion.6
  32.9 2.3 fusion.14
  35.2 5.1 %collective-permute-start.4 = (bf16[4,2,8,256]{3,2,1,0:T(8,128)(2,1)S(1)}, bf16[4,2,8,256]{3,2,1,0:T(8,128)(2,1)S(1)}, u32[]{:S(2)}, u32[]{:S(2)}) collective-permute-start(bf16[4,2,8,256]{3,2,1,0:T(8,128)(2,1)S(1)} %get-tuple-element.44), channel_id=1, source_target_pairs={{0,32},{32,64},{64,96},{96,128},{128,160},{160,192},{192,224},{1,3... | collective-permute-start | bytes 98312 | tf_op jit(solution)/shard_map/ppermute | solution.py:16
  40.4 1.9 collective-permute-start.5
  42.3 1.5 fusion.7
  43.8 2.4 collective-permute-done.5
  46.2 0.1 pad_maximum_fusion.6
  46.3 3.7 %collective-permute-start.6 = (bf16[4,20,2,256]{3,2,1,0:T(2,128)(2,1)S(1)}, bf16[4,20,2,256]{3,2,1,0:T(2,128)(2,1)S(1)}, u32[]{:S(2)}, u32[]{:S(2)}) collective-permute-start(bf16[4,20,2,256]{3,2,1,0:T(2,128)(2,1)S(1)} %get-tuple-element.37), channel_id=1, source_target_pairs={{1,0},{2,1},{3,2},{4,3},{5,4},{6,5},{7,6},{8,7},{9,8},{10,9},{11,1... | collective-permute-start | bytes 245768 | tf_op jit(solution)/shard_map/ppermute | solution.py:18
  50.0 2.0 collective-permute-done.6
  52.0 5.1 %collective-permute-done.7 = bf16[4,20,2,256]{3,2,1,0:T(2,128)(2,1)S(1)} collective-permute-done((bf16[4,20,2,256]{3,2,1,0:T(2,128)(2,1)S(1)}, bf16[4,20,2,256]{3,2,1,0:T(2,128)(2,1)S(1)}, u32[]{:S(2)}, u32[]{:S(2)}) %collective-permute-start.7) | collective-permute-done | bytes 81952 | tf_op jit(solution)/shard_map/ppermute | solution.py:16
  57.2 0.4 maximum_maximum_fusion.1
  57.6 0.1 fusion.9
  57.7 0.1 fusion.8
  57.8 0.0 copy-start.2
  58.0 1.0 copy-done.2
  59.1 0.8 fusion.5
  59.9 1.4 convolution_bitcast_fusion
  61.3 0.0 all-reduce.5.cloned.1.call-update
  61.3 1.4 add_convert_fusion
  62.8 115.5 %all-reduce.5.cloned.1.call-done = (f32[1024,256]{0,1:T(8,128)}, f32[2304,256]{1,0:T(8,128)}, f32[256,1024]{1,0:T(8,128)}) async-done(((f32[1024,256]{0,1:T(8,128)}, f32[2304,256]{1,0:T(8,128)}, f32[256,1024]{1,0:T(8,128)}), (f32[1024,256]{0,1:T(8,128)}, f32[2304,256]{1,0:T(8,128)}, f32[256,1024]{1,0:T(8,128)})) %all-reduce.5.cloned.1.call-update) | async-done | bytes 4456464 | tf_op jit(solution)/shard_map/psum | solution.py:119
  178.3 94.3 %all-reduce.6 = (bf16[1024,256]{0,1:T(8,128)(2,1)S(1)}, bf16[2304,256]{1,0:T(8,128)(2,1)}, bf16[256,1024]{1,0:T(8,128)(2,1)}) all-reduce(f32[1024,256]{0,1:T(8,128)} %get-tuple-element.16, f32[2304,256]{1,0:T(8,128)} %get-tuple-element.17, f32[256,1024]{1,0:T(8,128)} %get-tuple-element.18), channel_id=1, replica_groups=mesh['lat'=8,'lon'=32] {'lat'}, use_global_device_ids=true, to_apply=%region_2.3 | all-reduce | flops 1114112 | bytes 6684672 | tf_op jit(solution)/shard_map/psum | solution.py:119
  272.6 1.0 copy.23
  (41 shorter events, 0.5 us)
Async XLA Ops:
  7.2 1.0 copy-start
  7.2 171.1 %all-reduce.5.cloned.1.call-start = ((), (), s32[]{:S(2)}) async-start(), calls=%async_computation | async-start | bytes 8912896 | tf_op jit(solution)/shard_map/psum | solution.py:119
  8.2 7.7 %copy-start.4 = (s32[4,16,8]{1,2,0:T(8,128)S(1)}, s32[4,16,8]{1,2,0:T(8,128)}, u32[]{:S(2)}) copy-start(s32[4,16,8]{1,2,0:T(8,128)} %param.24) | copy-start | bytes 6148
  8.2 7.9 %copy-start.6 = (f32[3]{0:T(128)S(1)}, f32[3]{0:T(128)}, u32[]{:S(2)}) copy-start(f32[3]{0:T(128)} %param.25) | copy-start | bytes 40
  8.2 8.0 %copy-start.1 = (bf16[3,3,256,256]{3,2,1,0:T(8,128)(2,1)S(1)}, bf16[3,3,256,256]{3,2,1,0:T(8,128)(2,1)}, u32[]{:S(2)}) copy-start(bf16[3,3,256,256]{3,2,1,0:T(8,128)(2,1)} %param.17) | copy-start | bytes 3538948
  10.0 7.7 %collective-permute-start = (bf16[4,2,8,256]{3,2,1,0:T(8,128)(2,1)S(1)}, bf16[4,2,8,256]{3,2,1,0:T(8,128)(2,1)S(1)}, u32[]{:S(2)}, u32[]{:S(2)}) collective-permute-start(bf16[4,2,8,256]{3,2,1,0:T(8,128)(2,1)S(1)} %get-tuple-element.48), channel_id=1, source_target_pairs={{0,32},{32,64},{64,96},{96,128},{128,160},{160,192},{192,224},{1,3... | collective-permute-start | bytes 98312 | tf_op jit(solution)/shard_map/ppermute | solution.py:16
  13.9 6.9 %collective-permute-start.1 = (bf16[4,2,8,256]{3,2,1,0:T(8,128)(2,1)S(1)}, bf16[4,2,8,256]{3,2,1,0:T(8,128)(2,1)S(1)}, u32[]{:S(2)}, u32[]{:S(2)}) collective-permute-start(bf16[4,2,8,256]{3,2,1,0:T(8,128)(2,1)S(1)} %get-tuple-element.49), channel_id=1, source_target_pairs={{32,0},{64,32},{96,64},{128,96},{160,128},{192,160},{224,192},{33,... | collective-permute-start | bytes 98312 | tf_op jit(solution)/shard_map/ppermute | solution.py:18
  20.9 7.3 %collective-permute-start.2 = (bf16[4,20,2,256]{3,2,1,0:T(2,128)(2,1)S(1)}, bf16[4,20,2,256]{3,2,1,0:T(2,128)(2,1)S(1)}, u32[]{:S(2)}, u32[]{:S(2)}) collective-permute-start(bf16[4,20,2,256]{3,2,1,0:T(2,128)(2,1)S(1)} %get-tuple-element.41), channel_id=1, source_target_pairs={{0,1},{1,2},{2,3},{3,4},{4,5},{5,6},{6,7},{7,8},{8,9},{9,10},{10,1... | collective-permute-start | bytes 245768 | tf_op jit(solution)/shard_map/ppermute | solution.py:16
  21.0 7.2 %collective-permute-start.3 = (bf16[4,20,2,256]{3,2,1,0:T(2,128)(2,1)S(1)}, bf16[4,20,2,256]{3,2,1,0:T(2,128)(2,1)S(1)}, u32[]{:S(2)}, u32[]{:S(2)}) collective-permute-start(bf16[4,20,2,256]{3,2,1,0:T(2,128)(2,1)S(1)} %get-tuple-element.40), channel_id=1, source_target_pairs={{1,0},{2,1},{3,2},{4,3},{5,4},{6,5},{7,6},{8,7},{9,8},{10,9},{11,1... | collective-permute-start | bytes 245768 | tf_op jit(solution)/shard_map/ppermute | solution.py:18
  28.7 0.7 copy-start.10
  28.8 0.7 copy-start.11
  29.4 1.2 copy-start.3
  29.4 1.2 copy-start.5
  29.5 1.6 copy-start.7
  29.5 1.7 copy-start.8
  29.5 1.7 copy-start.9
  35.2 8.6 %collective-permute-start.4 = (bf16[4,2,8,256]{3,2,1,0:T(8,128)(2,1)S(1)}, bf16[4,2,8,256]{3,2,1,0:T(8,128)(2,1)S(1)}, u32[]{:S(2)}, u32[]{:S(2)}) collective-permute-start(bf16[4,2,8,256]{3,2,1,0:T(8,128)(2,1)S(1)} %get-tuple-element.44), channel_id=1, source_target_pairs={{0,32},{32,64},{64,96},{96,128},{128,160},{160,192},{192,224},{1,3... | collective-permute-start | bytes 98312 | tf_op jit(solution)/shard_map/ppermute | solution.py:16
  40.4 5.8 %collective-permute-start.5 = (bf16[4,2,8,256]{3,2,1,0:T(8,128)(2,1)S(1)}, bf16[4,2,8,256]{3,2,1,0:T(8,128)(2,1)S(1)}, u32[]{:S(2)}, u32[]{:S(2)}) collective-permute-start(bf16[4,2,8,256]{3,2,1,0:T(8,128)(2,1)S(1)} %get-tuple-element.45), channel_id=1, source_target_pairs={{32,0},{64,32},{96,64},{128,96},{160,128},{192,160},{224,192},{33,... | collective-permute-start | bytes 98312 | tf_op jit(solution)/shard_map/ppermute | solution.py:18
  46.3 5.8 %collective-permute-start.6 = (bf16[4,20,2,256]{3,2,1,0:T(2,128)(2,1)S(1)}, bf16[4,20,2,256]{3,2,1,0:T(2,128)(2,1)S(1)}, u32[]{:S(2)}, u32[]{:S(2)}) collective-permute-start(bf16[4,20,2,256]{3,2,1,0:T(2,128)(2,1)S(1)} %get-tuple-element.37), channel_id=1, source_target_pairs={{1,0},{2,1},{3,2},{4,3},{5,4},{6,5},{7,6},{8,7},{9,8},{10,9},{11,1... | collective-permute-start | bytes 245768 | tf_op jit(solution)/shard_map/ppermute | solution.py:18
  50.0 7.2 %collective-permute-start.7 = (bf16[4,20,2,256]{3,2,1,0:T(2,128)(2,1)S(1)}, bf16[4,20,2,256]{3,2,1,0:T(2,128)(2,1)S(1)}, u32[]{:S(2)}, u32[]{:S(2)}) collective-permute-start(bf16[4,20,2,256]{3,2,1,0:T(2,128)(2,1)S(1)} %get-tuple-element.36), channel_id=1, source_target_pairs={{0,1},{1,2},{2,3},{3,4},{4,5},{5,6},{6,7},{7,8},{8,9},{9,10},{10,1... | collective-permute-start | bytes 245768 | tf_op jit(solution)/shard_map/ppermute | solution.py:16
  57.8 1.3 copy-start.2
  57.8 1.3 copy-start.12
Sparse Core Ops, SparseCore 0:
  61.4 116.7 all-reduce.4
